TPU v7x, 512 devices: a whole 4x8x8 slice. The times are simulated.
512 devices in a mesh: chan: 128 (over y, z, core), seg: 4 (over x).
Axes of the slice: x: 4, y: 8, z: 8, core: 2. Of those that a mesh axis runs over, the one named last changes fastest.
Arguments:
- recording: float32 [16384, 16384], P('chan', 'seg'), may hold values from -60 to 60
- filter_taps: float32 [64], replicated, may hold values from -0.75 to 0.75
- offsets: int32 [4], replicated, may hold values from -64 to 64, as said below
- loop_partner: int32 [128, 3], replicated, may hold values from 0 to 127, as said below
- loop_count: int32 [128], replicated, may hold values from 0 to 3, as said below
Outputs:
- near_corr: float32 [16384, 4, 256], P('chan', 'seg')
- loop_corr: float32 [128, 3, 128, 256], P('chan', None, 'seg')
Inputs may be any that keep to these rules, and one draw needn't show every extreme that they name: 4 distinct nonzero offsets; both -64 and 64 are among them. `loop_partner`: slots at or beyond a block's loop_count are ignored. `loop_count`: some block uses all 3 slots.
All inputs are finite; a program needn't handle non-finite values.
Results may differ from a plain program's by a relative error of at most 0.004.
Values may be sent and summed in bfloat16 or wider, within the bound.
A program may use at most 64 MiB of HBM per device.

v0:
```python
import math

import jax
import jax.numpy as jnp
from jax import lax
from jax.sharding import PartitionSpec as P

NFFT = 1024
LAGS = 256
TAPS = 64
DECIM = 4
SPAN = 64
HALFBAND = 10
BINS = 512


WATER = 0.2
OUT_BLOCK = 128


def shifted(block, axis, distance):
    devices = range(lax.axis_size(axis))
    route = [(i - distance, i) for i in devices if i - distance in devices]
    return lax.ppermute(block, axis, route)


def with_halo(shard, sides, width):
    for axis, dim in sides:
        size, length = (lax.axis_size(axis), shard.shape[dim])
        up = [(i, (i + 1) % size) for i in range(size)]
        down = [(j, i) for i, j in up]
        last = lax.slice_in_dim(shard, length - width, length, axis=dim)
        initial = lax.slice_in_dim(shard, 0, width, axis=dim)
        before = lax.ppermute(last, axis, up)
        after = lax.ppermute(initial, axis, down)
        shard = jnp.concatenate([before, shard, after], axis=dim)
    return shard


def in_blocks(shard, dim, size):
    shape = shard.shape
    blocks = shard.reshape(*shape[:dim], size, shape[dim] // size, *shape[dim + 1 :])
    return jnp.moveaxis(blocks, dim, 0)


def summed_on_arrival(shard, axis, dim):
    size = lax.axis_size(axis)
    blocks = lax.all_to_all(in_blocks(shard, dim, size), axis, 0, 0, tiled=True)
    return jnp.sum(blocks, axis=0)


def tap_lookup(filter_taps, tap_index):
    valid = (tap_index >= 0) & (tap_index < TAPS)
    picked = filter_taps[jnp.clip(tap_index, 0, TAPS - 1)]
    return jnp.where(valid, picked, 0.0)


def decimate(recording, rim_samples, filter_taps):
    row_count = recording.shape[0]
    in_block = DECIM * OUT_BLOCK
    block_total = recording.shape[1] // in_block
    blocks = recording.reshape(row_count, block_total, in_block)
    tails = blocks[:, :, in_block - TAPS :]
    prior = jnp.concatenate([rim_samples[:, None, :], tails[:, : block_total - 1]], axis=1)
    outputs = jnp.arange(OUT_BLOCK, dtype=jnp.int32)
    main_pos = jnp.arange(in_block, dtype=jnp.int32)
    head_pos = jnp.arange(TAPS, dtype=jnp.int32) - TAPS
    main_table = tap_lookup(filter_taps, DECIM * outputs[None, :] + DECIM - 1 - main_pos[:, None])
    head_table = tap_lookup(filter_taps, DECIM * outputs[None, :] + DECIM - 1 - head_pos[:, None])
    high = lax.Precision.HIGHEST
    summed = jnp.einsum(
        "cbs,sq->cbq", blocks, main_table, precision=high, preferred_element_type=jnp.float32
    )
    summed = summed + jnp.einsum(
        "cbs,sq->cbq", prior, head_table, precision=high, preferred_element_type=jnp.float32
    )
    return summed.reshape(row_count, block_total * OUT_BLOCK)


def forward_table():
    column = jnp.arange(2 * BINS, dtype=jnp.int32)
    is_imag = column // BINS
    bin_index = column % BINS
    sample = jnp.arange(NFFT, dtype=jnp.int32)
    phase_idx = sample[:, None] * bin_index[None, :] % NFFT
    angles = phase_idx.astype(jnp.float32) * (2.0 * math.pi / NFFT)
    return jnp.where(is_imag[None, :] == 1, -jnp.sin(angles), jnp.cos(angles))


def inverse_table(total_segs):
    column = jnp.arange(2 * BINS, dtype=jnp.int32)
    is_imag = column // BINS
    bin_index = column % BINS
    lag_index = jnp.arange(LAGS, dtype=jnp.int32) - LAGS // 2
    phase_idx = bin_index[:, None] * lag_index[None, :] % NFFT
    angles = phase_idx.astype(jnp.float32) * (2.0 * math.pi / NFFT)
    weights = jnp.where(bin_index == 0, 1.0, 2.0) / math.sqrt(2.0 * BINS * total_segs)
    return jnp.where(is_imag[:, None] == 1, -jnp.sin(angles), jnp.cos(angles)) * weights[:, None]


def band_matrix():
    bin_ids = jnp.arange(BINS, dtype=jnp.int32)
    inside = (jnp.abs(bin_ids[:, None] - bin_ids[None, :]) <= HALFBAND).astype(jnp.float32)
    return inside / jnp.sum(inside, axis=0, keepdims=True)


def whiten(pieces):
    row_count = pieces.shape[0]
    spectrum = jnp.dot(
        pieces, forward_table(), precision=lax.Precision.HIGHEST, preferred_element_type=jnp.float32
    )
    parted = spectrum.reshape(row_count, 2, BINS)
    amplitude = jnp.sqrt(parted[:, 0] * parted[:, 0] + parted[:, 1] * parted[:, 1])
    smoothed = jnp.dot(
        amplitude,
        band_matrix(),
        precision=lax.Precision.HIGHEST,
        preferred_element_type=jnp.float32,
    )
    level_mean = jnp.mean(amplitude, axis=1, keepdims=True)
    divisor = smoothed + WATER * level_mean + 1e-06
    whitened = parted / divisor[:, None, :]
    return whitened.reshape(row_count, 2 * BINS).astype(jnp.bfloat16)


def cross(own, partner, form):
    full_width = own.shape[-1]
    half_width = full_width // 2
    own_real = own[..., :half_width]
    own_imag = own[..., half_width:]
    far_real = partner[..., :half_width]
    far_imag = partner[..., half_width:]
    wide = jnp.float32
    real_part = jnp.einsum(form, own_real, far_real, preferred_element_type=wide) + jnp.einsum(
        form, own_imag, far_imag, preferred_element_type=wide
    )
    imag_part = jnp.einsum(form, own_imag, far_real, preferred_element_type=wide) - jnp.einsum(
        form, own_real, far_imag, preferred_element_type=wide
    )
    return jnp.concatenate([real_part, imag_part], axis=-1)


def to_lags(pair_spec, inverse):
    lead_shape = pair_spec.shape[:-1]
    lag_rows = jnp.dot(
        pair_spec.reshape(-1, pair_spec.shape[-1]),
        inverse,
        precision=lax.Precision.HIGHEST,
        preferred_element_type=jnp.float32,
    )
    return lag_rows.reshape(lead_shape + (LAGS,))


def body(recording, filter_taps, offsets, loop_partner, loop_count):
    chan_count = lax.axis_size("chan")
    seg_count = lax.axis_size("seg")
    chan_rows = recording.shape[0]
    seg_local = recording.shape[1] // (DECIM * NFFT)
    total_segs = seg_local * seg_count
    bin_width = BINS // chan_count
    rim_samples = shifted(
        recording[:, recording.shape[1] - TAPS :].astype(jnp.bfloat16), "seg", 1
    ).astype(jnp.float32)
    decimated = decimate(recording, rim_samples, filter_taps)
    pieces = decimated.reshape(chan_rows, seg_local, NFFT)
    pieces = pieces - jnp.mean(pieces, axis=2, keepdims=True)
    whitened = whiten(pieces.reshape(chan_rows * seg_local, NFFT)).reshape(
        chan_rows, seg_local, 2 * BINS
    )
    inverse = inverse_table(total_segs)
    extended = with_halo(whitened, (("chan", 0),), SPAN)
    pick_rows = SPAN + offsets[:, None] + jnp.arange(chan_rows, dtype=jnp.int32)[None, :]
    near_partner = extended[pick_rows]
    near_spec = cross(whitened, near_partner, "cst,pcst->cpt")
    near_corr = summed_on_arrival(to_lags(near_spec, inverse), "seg", 1)
    bin_major = whitened.reshape(chan_rows, seg_local, 2, chan_count, bin_width)
    bin_major = jnp.transpose(bin_major, (3, 1, 2, 4, 0))[:, None]
    moved = lax.all_to_all(bin_major, "chan", split_axis=0, concat_axis=1, tiled=True)
    by_block = moved[0]
    partner_bins = by_block[loop_partner][..., ::-1]
    slot_ids = jnp.arange(loop_partner.shape[1], dtype=jnp.int32)
    live_slots = (slot_ids[None, :] < loop_count[:, None]).astype(jnp.float32)
    returned = lax.all_to_all(partner_bins, "chan", split_axis=0, concat_axis=4, tiled=True)
    partner_rows = jnp.transpose(returned[0], (4, 0, 1, 2, 3))
    partner_rows = partner_rows.reshape(chan_rows, partner_rows.shape[1], seg_local, 2 * BINS)
    partner_rows = jnp.transpose(partner_rows, (1, 0, 2, 3))
    own_live = lax.dynamic_index_in_dim(live_slots, lax.axis_index("chan"), 0, keepdims=False)
    loop_spec = cross(whitened, partner_rows, "cst,kcst->kct") * own_live[:, None, None]
    loop_corr = summed_on_arrival(to_lags(loop_spec, inverse), "seg", 1)
    loop_corr = loop_corr[None]
    return (near_corr, loop_corr)


def solution(mesh):
    in_specs = (P("chan", "seg"), P(), P(), P(), P())
    out_specs = (P("chan", "seg", None), P("chan", None, "seg", None))
    return jax.shard_map(body, mesh=mesh, in_specs=in_specs, out_specs=out_specs, check_vma=False)
```

profile of v0, /device:TPU:2, one launch (start us, length us, event | category | flops | bytes accessed | tf_op | source)
XLA Modules:
  0.0 230.0 jit_solution(11512676707876833320)
XLA Ops:
  0.6 0.0 copy-start
  0.6 1.9 copy.46
  2.6 3.4 %collective-permute-start = (bf16[128,64]{0,1:T(8,128)(2,1)S(1)}, bf16[128,64]{0,1:T(8,128)(2,1)S(1)}, u32[]{:S(2)}, u32[]{:S(2)}) collective-permute-start(bf16[128,64]{0,1:T(8,128)(2,1)S(1)} %slice.193), channel_id=1, source_target_pairs={{0,1},{1,2},{2,3},{4,5},{5,6},{6,7},{8,9},{9,10},{10,11},{12,13},{... | collective-permute-start | bytes 49160 | tf_op jit(solution)/shard_map/ppermute | solution.py:24
  6.0 0.0 copy-done
  6.0 0.7 fusion.532
  6.7 0.7 fusion.530
  7.5 0.7 fusion.531
  8.2 0.7 fusion.533
  8.9 0.1 fusion.422
  9.0 0.0 copy-start.2
  9.0 48.9 %gather_fusion = f32[8192]{0:T(1024)S(1)} fusion(f32[64]{0:T(128)S(1)} %copy-done, s32[8192]{0:T(1024)S(1)} %fusion.422), kind=kCustom, calls=%fused_computation | custom fusion | bytes 98304 | tf_op jit(solution)/shard_map/gather | solution.py:54
  57.9 0.0 copy-start.3
  57.9 0.0 copy-done.2
  58.0 0.1 copy.59
  58.1 0.2 reshape.507
  58.3 19.2 %fusion.540 = f32[2,512,1024]{2,1,0:T(8,128)} fusion(s32[2,512]{1,0:T(2,128)S(1)} %and_select_fusion, pred[2,512]{1,0:T(4,128)(4,1)S(1)} %fusion.440), kind=kLoop, calls=%fused_computation.10.clone.1 | loop fusion | flops 16777216 | bytes 4199424 | tf_op jit(solution)/shard_map/dot_general | solution.py:109
  77.5 0.0 copy-done.3
  77.5 0.6 dynamic-slice
  78.1 42.9 %convolution_bitcast_fusion = f32[128,8,128]{0,2,1:T(8,128)S(1)} fusion(f32[128,8,512]{0,2,1:T(8,128)S(1)} %bitcast.529, f32[]{:T(128)} %bitcast.114, f32[]{:T(128)} %bitcast.115, f32[]{:T(128)} %bitcast.116, f32[]{:T(128)} %bitcast.117, f32[]{:T(128)} %bitcast.118, f32[]{:T(128)} %bitcast.120, f32[]{:T(128)} %bitcast.119, f32[]{:T(128)} %bitcast.1, ...), kind=kOutput, calls=%fused_computation.44 | convolution fusion | flops 814219264 | bytes 2622208 | tf_op jit(solution)/shard_map/cbs,sq->cbq/dot_general | solution.py:71
  121.0 0.1 convert_reduce_fusion
  121.1 0.0 collective-permute-done
  121.1 0.8 fusion.534
  122.0 0.0 copy-done.1
  122.0 4.5 %fusion.3 = f32[128,2,512]{2,0,1:T(8,128)S(1)} fusion(f32[128,1024,1]{0,1,2:T(8,128)S(1)} %bitcast.530, f32[2,512,1024]{2,1,0:T(8,128)S(1)} %copy-done.1), kind=kOutput, calls=%fused_computation.9 | convolution fusion | flops 1610612736 | bytes 5242880 | tf_op jit(solution)/shard_map/dot_general | solution.py:109
  126.5 0.0 copy-start.4
  126.5 0.2 fusion.419
  126.7 0.7 fusion.31
  127.4 0.1 divide_convert_fusion
  127.5 0.2 copy.51
  127.7 0.8 copy.58
  128.5 17.8 %all-to-all-start.1 = ((bf16[128,1,1,2,4,128]{5,4,3,2,1,0:T(4,128)(2,1)}), bf16[128,1,1,2,4,128]{5,4,3,2,1,0:T(4,128)(2,1)S(1)}, u32[]{:S(2)}, u32[]{:S(2)}) async-start(bf16[128,1,1,2,4,128]{5,4,3,2,1,0:T(4,128)(2,1)} %copy.58), calls=%async_computation.1 | async-start | bytes 524288 | tf_op jit(solution)/shard_map/all_to_all | solution.py:178
  146.3 15.0 %all-to-all-done.1 = bf16[128,1,1,2,4,128]{5,4,3,2,1,0:T(4,128)(2,1)S(1)} async-done(((bf16[128,1,1,2,4,128]{5,4,3,2,1,0:T(4,128)(2,1)}), bf16[128,1,1,2,4,128]{5,4,3,2,1,0:T(4,128)(2,1)S(1)}, u32[]{:S(2)}, u32[]{:S(2)}) %all-to-all-start.1) | async-done | bytes 262176 | tf_op jit(solution)/shard_map/all_to_all | solution.py:178
  161.4 2.5 %gather_fusion.2 = bf16[384,2,4,128]{3,2,1,0:T(4,128)(2,1)S(1)} fusion(bf16[128,2,4,128]{3,2,1,0:T(4,128)(2,1)S(1)} %bitcast.524, s32[1024]{0:T(1024)S(1)} %pad_clamp_fusion), kind=kCustom, calls=%fused_computation.2 | custom fusion | bytes 1574400 | tf_op jit(solution)/shard_map/gather | solution.py:180
  163.9 3.3 %rev.3 = bf16[128,3,1,2,4,128]{5,4,3,1,0,2:T(4,128)(2,1)} reverse(bf16[128,3,1,2,4,128]{5,4,3,1,0,2:T(4,128)(2,1)S(1)} %bitcast.526), dimensions={5} | reverse | bytes 1572864 | tf_op jit(solution)/shard_map/rev | solution.py:180
  167.2 6.2 %all-to-all-start.2 = ((bf16[128,3,1,2,4,128]{5,4,3,1,2,0:T(4,128)(2,1)}), bf16[128,3,1,2,4,128]{5,4,3,1,2,0:T(4,128)(2,1)S(1)}, u32[]{:S(2)}, u32[]{:S(2)}) async-start(bf16[128,3,1,2,4,128]{5,4,3,1,2,0:T(4,128)(2,1)} %bitcast.154), calls=%async_computation.2 | async-start | bytes 1572864 | tf_op jit(solution)/shard_map/all_to_all | solution.py:183
  173.4 0.7 fusion.443
  174.1 0.1 fusion.442
  174.2 0.1 copy.50
  174.3 0.1 slice.56
  174.4 1.9 collective-permute-start.1
  176.3 0.1 copy.52
  176.5 0.1 slice.58
  176.6 7.0 %collective-permute-start.2 = (bf16[64,1,1024]{2,0,1:T(8,128)(2,1)S(1)}, bf16[64,1,1024]{2,0,1:T(8,128)(2,1)S(1)}, u32[]{:S(2)}, u32[]{:S(2)}) collective-permute-start(bf16[64,1,1024]{2,0,1:T(8,128)(2,1)S(1)} %slice.58), channel_id=1, source_target_pairs={{4,0},{8,4},{12,8},{16,12},{20,16},{24,20},{28,24},{32,28},{36,32}... | collective-permute-start | bytes 393224 | tf_op jit(solution)/shard_map/ppermute | solution.py:35
  183.5 0.1 copy.53
  183.7 0.1 copy.54
  183.9 0.1 copy.55
  184.0 13.2 %collective-permute-done.1 = bf16[64,1,1024]{2,0,1:T(8,128)(2,1)S(1)} collective-permute-done((bf16[64,1,1024]{2,0,1:T(8,128)(2,1)S(1)}, bf16[64,1,1024]{2,0,1:T(8,128)(2,1)S(1)}, u32[]{:S(2)}, u32[]{:S(2)}) %collective-permute-start.1) | collective-permute-done | bytes 131104 | tf_op jit(solution)/shard_map/ppermute | solution.py:34
  197.2 0.0 collective-permute-done.2
  197.2 2.1 gather_fusion.1
  199.3 0.3 fusion.33
  199.6 6.9 %fusion.27 = f32[4,128,1,256]{3,1,2,0:T(8,128)} fusion(f32[128,4,512]{2,0,1:T(8,128)S(1)} %get-tuple-element.3, f32[128,4,512]{2,0,1:T(8,128)S(1)} %get-tuple-element.2, f32[1024]{0:T(1024)S(1)} %select_multiply_fusion.3, s32[256]{0:T(256)S(1)} %iota_add_fusion, s32[1024]{0:T(1024)S(1)} %fusion.431, pred[1024]{0:T(1024)(128)(4,1)S(1)} %fusion.437), kind=kOutput, calls=%fused_computation.45 | convolution fusion | flops 1615593472 | bytes 2631680 | tf_op jit(solution)/shard_map/dot_general | solution.py:145
  206.5 0.0 all-to-all-done.2
  206.5 4.5 %all-to-all-start = ((f32[4,128,1,256]{3,1,2,0:T(8,128)}), f32[4,128,1,256]{3,1,2,0:T(8,128)S(1)}, u32[]{:S(2)}, u32[]{:S(2)}) async-start(f32[4,128,1,256]{3,1,2,0:T(8,128)} %fusion.27), calls=%async_computation | async-start | bytes 1048576 | tf_op jit(solution)/shard_map/all_to_all | solution.py:48
  211.0 0.3 copy.61
  211.3 0.2 fusion.41
  211.5 0.3 copy.62
  211.8 0.3 copy.63
  212.1 5.7 %fusion.30 = f32[4,3,32,256]{3,2,0,1:T(8,128)S(1)} fusion(f32[3,4,32,512]{3,2,1,0:T(8,128)S(1)} %bitcast.532, f32[3,4,32,512]{3,2,1,0:T(8,128)S(1)} %bitcast.531, f32[3]{0:T(128)S(1)} %fusion.443, f32[1024]{0:T(1024)S(1)} %select_multiply_fusion.3, s32[256]{0:T(256)S(1)} %iota_add_fusion, s32[1024]{0:T(1024)S(1)} %fusion.431, pred[1024]{0:T(1024)(128)(4,1)S(1)} %fusion.437), kind=kOutput, calls=%fused_computation.46 | convolution fusion | flops 1213202432 | bytes 1976332 | tf_op jit(solution)/shard_map/dot_general | solution.py:145
  217.8 0.8 copy.64
  218.6 0.0 all-to-all-done
  218.6 4.8 %all-to-all-start.3 = ((f32[4,3,32,256]{3,2,1,0:T(8,128)}), f32[4,3,32,256]{3,2,1,0:T(8,128)S(1)}, u32[]{:S(2)}, u32[]{:S(2)}) async-start(f32[4,3,32,256]{3,2,1,0:T(8,128)} %copy.64), calls=%async_computation.3 | async-start | bytes 786432 | tf_op jit(solution)/shard_map/all_to_all | solution.py:48
  223.4 0.7 reduce_sum.51
  224.2 5.1 %all-to-all-done.3 = f32[4,3,32,256]{3,2,1,0:T(8,128)S(1)} async-done(((f32[4,3,32,256]{3,2,1,0:T(8,128)}), f32[4,3,32,256]{3,2,1,0:T(8,128)S(1)}, u32[]{:S(2)}, u32[]{:S(2)}) %all-to-all-start.3) | async-done | bytes 393248 | tf_op jit(solution)/shard_map/all_to_all | solution.py:48
  229.3 0.7 reduce_sum.52
  (24 shorter events, 0.3 us)
Async XLA Ops:
  0.6 5.4 %copy-start = (f32[64]{0:T(128)S(1)}, f32[64]{0:T(128)}, u32[]{:S(2)}) copy-start(f32[64]{0:T(128)} %param.6) | copy-start | bytes 772
  2.6 118.5 %collective-permute-start = (bf16[128,64]{0,1:T(8,128)(2,1)S(1)}, bf16[128,64]{0,1:T(8,128)(2,1)S(1)}, u32[]{:S(2)}, u32[]{:S(2)}) collective-permute-start(bf16[128,64]{0,1:T(8,128)(2,1)S(1)} %slice.193), channel_id=1, source_target_pairs={{0,1},{1,2},{2,3},{4,5},{5,6},{6,7},{8,9},{9,10},{10,11},{12,13},{... | collective-permute-start | bytes 49160 | tf_op jit(solution)/shard_map/ppermute | solution.py:24
  9.0 48.9 %copy-start.2 = (s32[128,3]{0,1:T(4,128)S(1)}, s32[128,3]{0,1:T(4,128)}, u32[]{:S(2)}) copy-start(s32[128,3]{0,1:T(4,128)} %param.8) | copy-start | bytes 4612
  57.9 19.5 %copy-start.3 = (s32[128]{0:T(128)S(1)}, s32[128]{0:T(128)}, u32[]{:S(2)}) copy-start(s32[128]{0:T(128)} %param.9) | copy-start | bytes 1540
  78.1 43.9 %copy-start.1 = (f32[2,512,1024]{2,1,0:T(8,128)S(1)}, f32[2,512,1024]{2,1,0:T(8,128)}, u32[]{:S(2)}) copy-start(f32[2,512,1024]{2,1,0:T(8,128)} %fusion.540) | copy-start | bytes 12582916
  126.5 19.9 %copy-start.4 = (s32[4]{0:T(128)S(1)}, s32[4]{0:T(128)}, u32[]{:S(2)}) copy-start(s32[4]{0:T(128)} %param.7) | copy-start | bytes 52
  128.5 32.9 %all-to-all-start.1 = ((bf16[128,1,1,2,4,128]{5,4,3,2,1,0:T(4,128)(2,1)}), bf16[128,1,1,2,4,128]{5,4,3,2,1,0:T(4,128)(2,1)S(1)}, u32[]{:S(2)}, u32[]{:S(2)}) async-start(bf16[128,1,1,2,4,128]{5,4,3,2,1,0:T(4,128)(2,1)} %copy.58), calls=%async_computation.1 | async-start | bytes 524288 | tf_op jit(solution)/shard_map/all_to_all | solution.py:178
  167.2 39.3 %all-to-all-start.2 = ((bf16[128,3,1,2,4,128]{5,4,3,1,2,0:T(4,128)(2,1)}), bf16[128,3,1,2,4,128]{5,4,3,1,2,0:T(4,128)(2,1)S(1)}, u32[]{:S(2)}, u32[]{:S(2)}) async-start(bf16[128,3,1,2,4,128]{5,4,3,1,2,0:T(4,128)(2,1)} %bitcast.154), calls=%async_computation.2 | async-start | bytes 1572864 | tf_op jit(solution)/shard_map/all_to_all | solution.py:183
  174.4 22.8 %collective-permute-start.1 = (bf16[64,1,1024]{2,0,1:T(8,128)(2,1)S(1)}, bf16[64,1,1024]{2,0,1:T(8,128)(2,1)S(1)}, u32[]{:S(2)}, u32[]{:S(2)}) collective-permute-start(bf16[64,1,1024]{2,0,1:T(8,128)(2,1)S(1)} %slice.56), channel_id=1, source_target_pairs={{0,4},{4,8},{8,12},{12,16},{16,20},{20,24},{24,28},{28,32},{32,36}... | collective-permute-start | bytes 393224 | tf_op jit(solution)/shard_map/ppermute | solution.py:34
  176.6 20.6 %collective-permute-start.2 = (bf16[64,1,1024]{2,0,1:T(8,128)(2,1)S(1)}, bf16[64,1,1024]{2,0,1:T(8,128)(2,1)S(1)}, u32[]{:S(2)}, u32[]{:S(2)}) collective-permute-start(bf16[64,1,1024]{2,0,1:T(8,128)(2,1)S(1)} %slice.58), channel_id=1, source_target_pairs={{4,0},{8,4},{12,8},{16,12},{20,16},{24,20},{28,24},{32,28},{36,32}... | collective-permute-start | bytes 393224 | tf_op jit(solution)/shard_map/ppermute | solution.py:35
  206.5 12.1 %all-to-all-start = ((f32[4,128,1,256]{3,1,2,0:T(8,128)}), f32[4,128,1,256]{3,1,2,0:T(8,128)S(1)}, u32[]{:S(2)}, u32[]{:S(2)}) async-start(f32[4,128,1,256]{3,1,2,0:T(8,128)} %fusion.27), calls=%async_computation | async-start | bytes 1048576 | tf_op jit(solution)/shard_map/all_to_all | solution.py:48
  218.6 10.7 %all-to-all-start.3 = ((f32[4,3,32,256]{3,2,1,0:T(8,128)}), f32[4,3,32,256]{3,2,1,0:T(8,128)S(1)}, u32[]{:S(2)}, u32[]{:S(2)}) async-start(f32[4,3,32,256]{3,2,1,0:T(8,128)} %copy.64), calls=%async_computation.3 | async-start | bytes 786432 | tf_op jit(solution)/shard_map/all_to_all | solution.py:48
where the time goes:
time: 231 us; the launch traced here: 230 us
  local copies, waits for them, and re-layouts  66.7 us (29%)
  matrix products  61.5 us (27%)
  starting transfers between devices  45.6 us (20%)
  waiting for transfers between devices  33.3 us (14%)
  other arithmetic  21.8 us (9%)
    gather x5, local copies, waits for them, and re-layouts, tap_lookup(): picked = filter_taps[jnp.clip(tap_index, 0, TAPS - 1)]  51.7 us
    dot_general x1, matrix products, decimate(): jnp.einsum('cbs,sq->cbq', blocks, main_table, precision=high, preferred_e...  42.9 us
    dot_general x1, other arithmetic, whiten(): jnp.dot(pieces, forward_table(), precision=lax.Precision.HIGHEST, preferr...  19.2 us
    all_to_all x1, starting transfers between devices, body(): lax.all_to_all(bin_major, 'chan', split_axis=0, concat_axis=1, tiled=True)  17.8 us
    all_to_all x1, waiting for transfers between devices, body(): lax.all_to_all(bin_major, 'chan', split_axis=0, concat_axis=1, tiled=True)  15 us
    ppermute x1, waiting for transfers between devices, with_halo(): before = lax.ppermute(last, axis, up)  13.2 us
    dot_general x2, matrix products, to_lags(): jnp.dot(pair_spec.reshape(-1, pair_spec.shape[-1]), inverse, precision=la...  12.6 us
    all_to_all x2, starting transfers between devices, summed_on_arrival(): blocks = lax.all_to_all(in_blocks(shard, dim, size), axis, 0, 0, tiled=True)  9.33 us
  transfers between devices with their start and end apart: 7, of which 3 were waited for; matrix products, arithmetic and copies ran while one was open for 58% of the time, Pallas kernels for 0%

commit v1 on v0

v1 whole, which is shorter than its diff:
```python
import math

import jax
import jax.numpy as jnp
import numpy as np
from jax import lax
from jax.experimental import pallas as pl
from jax.experimental.pallas import tpu as pltpu
from jax.sharding import PartitionSpec as P

C = 128
NOFF = 4
NFFT = 1024
LAGS = 256
TAPS = 64
DECIM = 4
HALFBAND = 10
BINS = 512
MAXLB = 3
SEGS = 4
WATER = 0.2
X, Y, ZC = 4, 8, 16
XY = X * Y
RIM = 128
QB = 128
WIN = DECIM * QB + RIM
NB = NFFT // QB
MESH = pl.DeviceIdType.MESH
BF = jnp.bfloat16
F32 = jnp.float32


def split_np(a):
    hi = a.astype(np.float32).astype(jnp.bfloat16)
    lo = (a - hi.astype(np.float64)).astype(np.float32).astype(jnp.bfloat16)
    return hi, lo


def bin_order():
    p = np.arange(BINS)
    return np.where(p < BINS // 2, 2 * p, 2 * (p - BINS // 2) + 1)


def forward_tables():
    sample = np.arange(NFFT // 2)
    out = []
    for odd in range(2):
        bins = 2 * np.arange(BINS // 2) + odd
        angle = 2.0 * np.pi * (bins[:, None] * sample[None, :] % NFFT) / NFFT
        real = np.cos(angle) * (bins[:, None] > 0)
        out.extend(split_np(np.concatenate([real, -np.sin(angle)], axis=0)))
    return np.stack(out)


def lag_tables():
    bins = bin_order()
    lag = np.arange(LAGS) - LAGS // 2
    angle = 2.0 * np.pi * (bins[None, :] * lag[:, None] % NFFT) / NFFT
    weight = np.where(bins == 0, 1.0, 2.0) / math.sqrt(2.0 * BINS * SEGS)
    both = np.concatenate([np.cos(angle) * weight, -np.sin(angle) * weight], axis=1)
    return np.stack(split_np(both))


def dot(a, b):
    return jnp.dot(a, b, preferred_element_type=F32)


def dot_nt(a, b):
    return lax.dot_general(a, b, (((1,), (1,)), ((), ())), preferred_element_type=F32)


def halves(a):
    hi = a.astype(BF)
    return hi, (a - hi.astype(F32)).astype(BF)


def iota(shape, dim):
    return lax.broadcasted_iota(jnp.int32, shape, dim)


def where_am_i():
    chan = lax.axis_index("chan")
    return lax.axis_index("seg"), chan // ZC, lax.rem(chan, ZC)


def kernel(
    off_ref, rec_hbm, taps_ref, part_ref, count_ref, fwd_hbm, lag_hbm,
    near_out, loop_out,
    raw, rec, dec, fwd, lagt, perm, permt, band, rim_send, rim_recv,
    spec, uv, white_a, white_b, halo_send, halo_recv,
    a1, a2, a3, b1, b2, b3, wr, wi, a4, a5, b4, b5, near_part, near_send, near_recv, back_a, back_b,
    local_sem, rim_sem, halo_sem, near_sem, ssem, rsem,
):
    x, y, zc = where_am_i()
    chan = lax.axis_index("chan")

    def zc_dev(i):
        return (y * ZC + i, x)

    def xy_dev(i):
        return (lax.rem(i, Y) * ZC + zc, i // Y)

    me_xy = x * Y + y
    before = (lax.rem(chan + C - 1, C), x)
    after = (lax.rem(chan + 1, C), x)

    loads = []
    order = [NB - 1] + list(range(NB - 1))
    for n, b in enumerate(order):
        cols = pl.ds(b * DECIM * QB, DECIM * QB)
        loads.append(pltpu.make_async_copy(rec_hbm.at[:, cols], raw.at[:, cols], local_sem.at[n]))
    load_fwd = pltpu.make_async_copy(fwd_hbm, fwd, local_sem.at[NB])
    load_lag = pltpu.make_async_copy(lag_hbm, lagt, local_sem.at[NB + 1])
    for c in loads:
        c.start()
    load_fwd.start()
    load_lag.start()

    barrier = pltpu.get_barrier_semaphore()

    def signal_zc(i, _):
        pl.semaphore_signal(barrier, inc=1, device_id=zc_dev(lax.rem(zc + i, ZC)), device_id_type=MESH)
        return 0

    def signal_xy(i, _):
        pl.semaphore_signal(barrier, inc=1, device_id=xy_dev(lax.rem(me_xy + i, XY)), device_id_type=MESH)
        return 0

    lax.fori_loop(1, ZC, signal_zc, 0)
    lax.fori_loop(1, XY, signal_xy, 0)
    pl.semaphore_signal(barrier, inc=1, device_id=before, device_id_type=MESH)
    pl.semaphore_signal(barrier, inc=1, device_id=after, device_id_type=MESH)

    r = iota((BINS, BINS), 0)
    c = iota((BINS, BINS), 1)
    perm[...] = jnp.where(c == lax.rem(r, ZC) * XY + r // ZC, 1.0, 0.0).astype(BF)
    permt[...] = jnp.where(c == lax.rem(r, XY) * ZC + r // XY, 1.0, 0.0).astype(BF)
    half = BINS // 2
    fr = jnp.where(r < half, 2 * r, 2 * (r - half) + 1)
    fc = jnp.where(c < half, 2 * c, 2 * (c - half) + 1)
    band[...] = jnp.where(jnp.abs(fr - fc) <= HALFBAND, 1.0, 0.0).astype(BF)

    place = (iota((TAPS, WIN), 1) == 67 + TAPS - iota((TAPS, WIN), 0))
    place = jnp.where(place, 1.0, 0.0).astype(BF)
    t_hi, t_lo = halves(jnp.broadcast_to(taps_ref[...], (8, TAPS)))
    row_hi = jnp.broadcast_to(dot(t_hi, place)[0:1], (QB, WIN))
    row_lo = jnp.broadcast_to(dot(t_lo, place)[0:1], (QB, WIN))
    tab_hi = pltpu.roll(row_hi, 0, 1, stride=DECIM, stride_axis=0).astype(BF)
    tab_lo = pltpu.roll(row_lo, 0, 1, stride=DECIM, stride_axis=0).astype(BF)

    def take(n):
        b = order[n]
        loads[n].wait()
        cols = pl.ds(b * DECIM * QB, DECIM * QB)
        hi, lo = halves(raw[:, cols])
        to = pl.ds(RIM + b * DECIM * QB, DECIM * QB)
        rec[0:C, to] = hi
        rec[C : 2 * C, to] = lo

    def decimate(b):
        win = pl.ds(b * DECIM * QB, WIN)
        both = dot_nt(tab_hi, rec[:, win])
        out = both[:, :C] + both[:, C:] + dot_nt(tab_lo, rec[0:C, win])
        dec[b * QB : (b + 1) * QB, :] = out

    take(0)
    rim_send[...] = raw[:, NFFT * DECIM - RIM :].astype(BF)
    for n in range(1, NB):
        take(n)
        if order[n] > 0:
            decimate(order[n])
    decimate(NB - 1)

    pl.semaphore_wait(barrier, ZC - 1 + XY - 1 + 2)
    rim = pltpu.make_async_remote_copy(
        rim_send, rim_recv, rim_sem.at[0], rim_sem.at[1],
        device_id=(chan, lax.rem(x + 1, X)), device_id_type=MESH,
    )
    rim.start()

    level = jnp.sum(dec[QB:, :], axis=0, keepdims=True) * (1.0 / (NFFT - QB))

    def fold(lo_row, hi_row):
        low = dec[lo_row:hi_row, :] - level
        high = dec[lo_row + NFFT // 2 : hi_row + NFFT // 2, :] - level
        for k, v in enumerate((low + high, low - high)):
            hi, lo = halves(v)
            uv[k, lo_row:hi_row, 0:C] = hi
            uv[k, lo_row:hi_row, C : 2 * C] = lo

    def transform(lo_row, hi_row):
        outs = []
        for k in range(2):
            v = uv[k, lo_row:hi_row, :]
            both = dot(fwd[2 * k, :, lo_row:hi_row], v)
            outs.append(both[:, :C] + both[:, C:] + dot(fwd[2 * k + 1, :, lo_row:hi_row], v[:, :C]))
        return outs

    fold(QB, NFFT // 2)
    load_fwd.wait()
    for k, s in enumerate(transform(QB, NFFT // 2)):
        spec[k] = s

    rim.wait()
    inside = (iota((C, RIM), 1) >= RIM - TAPS) & (x > 0)
    rec[0:C, 0:RIM] = jnp.where(inside, rim_recv[...].astype(F32), 0.0).astype(BF)
    rec[C : 2 * C, 0:RIM] = jnp.zeros((C, RIM), BF)
    decimate(0)
    fold(0, QB)
    for k, s in enumerate(transform(0, QB)):
        spec[k] = spec[k] + s

    real = jnp.concatenate([spec[0, :half, :], spec[1, :half, :]], axis=0)
    imag = jnp.concatenate([spec[0, half:, :], spec[1, half:, :]], axis=0)
    amp = jnp.sqrt(real * real + imag * imag)
    amp_hi, amp_lo = halves(amp)
    near_sum = dot(band[...], amp_hi) + dot(band[...], amp_lo)
    rows = iota((BINS, C), 0)
    f = jnp.where(rows < half, 2 * rows, 2 * (rows - half) + 1)
    width = jnp.minimum(f, HALFBAND) + jnp.minimum(BINS - 1 - f, HALFBAND) + 1
    mean_amp = jnp.sum(amp, axis=0, keepdims=True) * (1.0 / BINS)
    divisor = near_sum / width.astype(F32) + WATER * mean_amp + 1e-06
    wre = (real / divisor).astype(BF)
    wim = (imag / divisor).astype(BF)
    white_a[...] = wre
    white_b[...] = dot(perm[...], wim).astype(BF)

    def send_zc(src, dst, k):
        def body(i, _):
            d = lax.rem(zc + i, ZC)
            pltpu.make_async_remote_copy(
                src.at[pl.ds(d * XY, XY)], dst.at[pl.ds(zc * XY, XY)], ssem.at[k], rsem.at[k],
                device_id=zc_dev(d), device_id_type=MESH,
            ).start()
            return 0

        lax.fori_loop(1, ZC, body, 0)
        mine = pl.ds(pl.multiple_of(zc * XY, XY), XY)
        dst[mine, :] = src[mine, :]

    def send_xy(src, dst, k):
        def body(i, _):
            d = lax.rem(me_xy + i, XY)
            pltpu.make_async_remote_copy(
                src.at[pl.ds(d * ZC, ZC)], dst.at[pl.ds(me_xy * ZC, ZC)], ssem.at[k], rsem.at[k],
                device_id=xy_dev(d), device_id_type=MESH,
            ).start()
            return 0

        lax.fori_loop(1, XY, body, 0)
        mine = pl.ds(pl.multiple_of(me_xy * ZC, ZC), ZC)
        dst[mine, :] = src[mine, :]

    def done(ref, sems, k, count):
        part = ref.at[pl.ds(0, count)]
        pltpu.make_async_copy(part, part, sems.at[k]).wait()

    zc_rows = (ZC - 1) * XY
    xy_rows = (XY - 1) * ZC

    send_zc(white_a, a1, 0)
    send_xy(white_b, b1, 1)

    lane = iota((BINS, C), 1)
    left = lane < 64
    wre = wre.astype(F32)
    wim = wim.astype(F32)
    halo_send[0] = jnp.where(left, wre, pltpu.roll(wim, 64, 1)).astype(BF)
    halo_send[1] = jnp.where(left, pltpu.roll(wre, 64, 1), wim).astype(BF)
    to_before = pltpu.make_async_remote_copy(
        halo_send.at[0], halo_recv.at[0], halo_sem.at[0], halo_sem.at[1],
        device_id=before, device_id_type=MESH,
    )
    to_after = pltpu.make_async_remote_copy(
        halo_send.at[1], halo_recv.at[1], halo_sem.at[2], halo_sem.at[3],
        device_id=after, device_id_type=MESH,
    )
    to_before.start()
    to_after.start()
    to_before.wait()
    to_after.wait()
    load_lag.wait()

    def near(o, _):
        off = off_ref[o]
        own_r = white_a[...].astype(F32)
        own_i = wim
        nxt = halo_recv[0].astype(F32)
        prv = halo_recv[1].astype(F32)
        far_r = jnp.where(left, nxt, pltpu.roll(prv, 64, 1))
        far_i = jnp.where(left, pltpu.roll(nxt, 64, 1), prv)
        src = lane - off
        keep = (src >= 0) & (src < C)
        turn = lax.rem(C - off, C)
        pr = pltpu.roll(jnp.where(keep, own_r, far_r), turn, 1)
        pi = pltpu.roll(jnp.where(keep, own_i, far_i), turn, 1)
        sr = own_r * pr + own_i * pi
        si = own_i * pr - own_r * pi
        out = jnp.zeros((LAGS, C), F32)
        for k, s in enumerate((sr, si)):
            hi, lo = halves(s)
            cols = slice(k * BINS, (k + 1) * BINS)
            out = out + dot(lagt[0, :, cols], hi) + dot(lagt[0, :, cols], lo) + dot(lagt[1, :, cols], hi)
        near_part[o] = out
        near_send[o] = out.astype(BF)
        return 0

    lax.fori_loop(0, 2, near, 0)

    done(a1, rsem, 0, zc_rows)
    a2[...] = dot(perm[...], a1[...]).astype(BF)
    send_xy(a2, wr, 2)
    done(b1, rsem, 1, xy_rows)
    b2[...] = dot(permt[...], b1[...]).astype(BF)
    send_zc(b2, b3, 3)

    lax.fori_loop(2, NOFF, near, 0)

    def near_to(i, k):
        d = lax.rem(x + i, X)
        return pltpu.make_async_remote_copy(
            near_send.at[d], near_recv.at[i - 1], near_sem.at[0], near_sem.at[1],
            device_id=(chan, d), device_id_type=MESH,
        )

    for i in range(1, X):
        near_to(i, 0).start()

    lane_b = iota((C, C), 1)
    row_b = iota((C, C), 0)
    flip = jnp.where(lane_b + row_b == C - 1, 1.0, 0.0).astype(BF)
    picks = []
    for k in range(MAXLB):
        line = jnp.where(count_ref[...] > k, part_ref[k : k + 1, :], -1).astype(F32)
        column = jnp.sum(jnp.where(lane_b == row_b, jnp.broadcast_to(line, (C, C)), 0.0), axis=1, keepdims=True)
        picks.append(jnp.where(column == lane_b.astype(F32), 1.0, 0.0).astype(BF))
    pick = jnp.concatenate(picks, axis=0)

    done(wr, rsem, 2, xy_rows)
    done(b3, rsem, 3, zc_rows)
    wi[...] = dot(perm[...], b3[...]).astype(BF)

    loop_r = [jnp.zeros((C, C), F32) for _ in range(MAXLB)]
    loop_i = [jnp.zeros((C, C), F32) for _ in range(MAXLB)]
    for s in range(SEGS):
        own_r = wr[s * C : (s + 1) * C, :]
        own_i = wi[s * C : (s + 1) * C, :]
        far_r = dot(pick, dot(own_r, flip).astype(BF))
        far_i = dot(pick, dot(own_i, flip).astype(BF))
        own_r = own_r.astype(F32)
        own_i = own_i.astype(F32)
        for k in range(MAXLB):
            pr = far_r[k * C : (k + 1) * C, :]
            pi = far_i[k * C : (k + 1) * C, :]
            loop_r[k] = loop_r[k] + own_r * pr + own_i * pi
            loop_i[k] = loop_i[k] + own_i * pr - own_r * pi

    def gather_lanes(parts, q):
        out = jnp.zeros((C, C), F32)
        for j, p in enumerate(parts):
            turned = p if j == q else pltpu.roll(p, 32 * ((j - q) % 4), 1)
            out = jnp.where((lane_b >= 32 * j) & (lane_b < 32 * (j + 1)), turned, out)
        return out.astype(BF)

    for q in range(X):
        rows = slice(q * C, (q + 1) * C)
        back_a[rows, :] = gather_lanes([loop_r[0], loop_i[0], loop_r[1], loop_i[1]], q)
        back_b[rows, :] = gather_lanes([loop_r[2], loop_i[2]], q)

    done(a2, ssem, 2, xy_rows)
    done(b2, ssem, 3, zc_rows)
    done(white_a, ssem, 0, zc_rows)
    done(white_b, ssem, 1, xy_rows)
    a3[...] = dot(permt[...], back_a[...]).astype(BF)
    send_zc(a3, a4, 4)
    send_xy(back_b, b4, 5)

    three = near_recv.at[pl.ds(0, X - 1)]
    pltpu.make_async_copy(three, three, near_sem.at[1]).wait()
    total = near_part[x]
    for i in range(X - 1):
        total = total + near_recv[i].astype(F32)
    near_out[...] = jnp.transpose(total)

    done(a4, rsem, 4, zc_rows)
    a2[...] = dot(perm[...], a4[...]).astype(BF)
    send_xy(a2, a5, 6)
    done(b4, rsem, 5, xy_rows)
    b2[...] = dot(permt[...], b4[...]).astype(BF)
    send_zc(b2, b5, 7)

    done(a5, rsem, 6, xy_rows)
    got_a = dot(permt[...], a5[...]).astype(BF)
    lag_r = dot(lagt[0, :, :BINS], got_a) + dot(lagt[1, :, :BINS], got_a)
    lag_i = dot(lagt[0, :, BINS:], got_a) + dot(lagt[1, :, BINS:], got_a)
    lag_r = jnp.transpose(lag_r)
    lag_i = jnp.transpose(lag_i)
    loop_out[0] = lag_r[0:32] + lag_i[32:64]
    loop_out[1] = lag_r[64:96] + lag_i[96:128]
    done(b5, rsem, 7, zc_rows)
    got_b = b5[...]
    lag_r = dot(lagt[0, :, :BINS], got_b) + dot(lagt[1, :, :BINS], got_b)
    lag_i = dot(lagt[0, :, BINS:], got_b) + dot(lagt[1, :, BINS:], got_b)
    lag_r = jnp.transpose(lag_r)
    lag_i = jnp.transpose(lag_i)
    loop_out[2] = lag_r[0:32] + lag_i[32:64]

    pltpu.make_async_copy(three, three, near_sem.at[0]).wait()
    done(a3, ssem, 4, zc_rows)
    done(back_b, ssem, 5, xy_rows)
    done(a2, ssem, 6, xy_rows)
    done(b2, ssem, 7, zc_rows)


def body(recording, filter_taps, offsets, loop_partner, loop_count):
    fwd = jnp.asarray(forward_tables())
    lagt = jnp.asarray(lag_tables())
    vmem = pl.BlockSpec(memory_space=pltpu.VMEM)
    hbm = pl.BlockSpec(memory_space=pl.ANY)
    smem = pl.BlockSpec(memory_space=pltpu.SMEM)
    rows = pltpu.VMEM((BINS, C), BF)
    dma = pltpu.SemaphoreType.DMA
    near, loop = pl.pallas_call(
        kernel,
        out_shape=(
            jax.ShapeDtypeStruct((C, LAGS), F32),
            jax.ShapeDtypeStruct((MAXLB, C // X, LAGS), F32),
        ),
        in_specs=[smem, hbm, vmem, vmem, vmem, hbm, hbm],
        out_specs=(vmem, vmem),
        scratch_shapes=[
            pltpu.VMEM((C, NFFT * DECIM), F32),
            pltpu.VMEM((2 * C, RIM + NFFT * DECIM), BF),
            pltpu.VMEM((NFFT, C), F32),
            pltpu.VMEM((4, BINS, NFFT // 2), BF),
            pltpu.VMEM((2, LAGS, 2 * BINS), BF),
            pltpu.VMEM((BINS, BINS), BF),
            pltpu.VMEM((BINS, BINS), BF),
            pltpu.VMEM((BINS, BINS), BF),
            pltpu.VMEM((C, RIM), BF),
            pltpu.VMEM((C, RIM), BF),
            pltpu.VMEM((2, BINS, C), F32),
            pltpu.VMEM((2, NFFT // 2, 2 * C), BF),
            rows, rows,
            pltpu.VMEM((2, BINS, C), BF),
            pltpu.VMEM((2, BINS, C), BF),
            rows, rows, rows, rows, rows, rows, rows, rows, rows, rows, rows, rows,
            pltpu.VMEM((NOFF, LAGS, C), F32),
            pltpu.VMEM((NOFF, LAGS, C), BF),
            pltpu.VMEM((X - 1, LAGS, C), BF),
            rows, rows,
            dma((NB + 2,)), dma((2,)), dma((4,)), dma((2,)), dma((8,)), dma((8,)),
        ],
        compiler_params=pltpu.CompilerParams(collective_id=0, has_side_effects=True),
    )(
        offsets, recording, filter_taps.reshape(1, TAPS), loop_partner.T,
        loop_count.reshape(1, C), fwd, lagt,
    )
    return near[:, None, :], loop[None]


def solution(mesh):
    in_specs = (P("chan", "seg"), P(), P(), P(), P())
    out_specs = (P("chan", "seg", None), P("chan", None, "seg", None))
    return jax.shard_map(body, mesh=mesh, in_specs=in_specs, out_specs=out_specs, check_vma=False)
```

time: 231 us -> 58.4 us (0.25)
  the two profiles are of different devices: /device:TPU:2 before, /device:TPU:1 now
where the time goes in v1:
time: 58.4 us; the launch traced here: 58.2 us
  Pallas kernels  54.3 us (93%)
  local copies, waits for them, and re-layouts  3.23 us (6%)
  between operations  0.64 us (1%)
    pallas_call x1, Pallas kernels, body(): pl.pallas_call(kernel, out_shape=(jax.ShapeDtypeStruct((C, LAGS), F32), j...  54.3 us
    unnamed x2, local copies, waits for them, and re-layouts  3.23 us

profile of v1, /device:TPU:1, one launch (start us, length us, event | category | flops | bytes accessed | tf_op | source)
XLA Modules:
  0.0 58.2 jit_solution(11370736379466628713)
XLA Ops:
  0.6 54.3 %shard_map.86 = (f32[128,256]{1,0:T(8,128)}, f32[3,32,256]{2,1,0:T(8,128)}) custom-call(s32[4]{0:T(128)} %off_ref.1, f32[128,4096]{1,0:T(8,128)} %rec_hbm.1, f32[1,64]{1,0:T(1,128)} %bitcast.8, s32[3,128]{1,0:T(4,128)} %bitcast.7, s32[1,128]{1,0:T(1,128)} %bitcast.9, bf16[4,512,512]{2,1,0:T(8,128)(2,1)} %constant.4.clone.fwd_hbm, ...), custom_call_target="tpu_custom_call" | custom-call | tf_op jit(solution)/shard_map/pallas_call | solution.py:423
  55.0 1.7 %copy.9 = f32[128,1,256]{2,1,0:T(1,128)} copy(f32[128,1,256]{2,0,1:T(8,128)} %bitcast.5) | data formatting | bytes 262144
  56.7 1.5 %copy.11 = f32[1,3,32,256]{3,2,1,0:T(8,128)} copy(f32[1,3,32,256]{3,2,1,0:T(8,128)} %bitcast.6) | data formatting | bytes 196608

commit v2 on v1

--- a/solution.py
+++ b/solution.py
@@ -78,29 +78,63 @@
     return lax.broadcasted_iota(jnp.int32, shape, dim)
 
 
+def wrap(v, n):
+    v = jnp.where(v >= n, v - n, v)
+    return jnp.where(v < 0, v + n, v)
+
+
 def where_am_i():
     chan = lax.axis_index("chan")
     return lax.axis_index("seg"), chan // ZC, lax.rem(chan, ZC)
 
 
 def kernel(
-    off_ref, rec_hbm, taps_ref, part_ref, count_ref, fwd_hbm, lag_hbm,
+    off_hbm, rec_hbm, taps_hbm, part_hbm, count_hbm, fwd_hbm, lag_hbm,
     near_out, loop_out,
+    off_ref, taps_ref, part_ref, count_ref,
     raw, rec, dec, fwd, lagt, perm, permt, band, rim_send, rim_recv,
     spec, uv, white_a, white_b, halo_send, halo_recv,
     a1, a2, a3, b1, b2, b3, wr, wi, a4, a5, b4, b5, near_part, near_send, near_recv, back_a, back_b,
-    local_sem, rim_sem, halo_sem, near_sem, ssem, rsem,
+    local_sem, small_sem, rim_sem, halo_sem, near_sem, ssem, rsem,
 ):
     x, y, zc = where_am_i()
     chan = lax.axis_index("chan")
 
-    def zc_dev(i):
-        return (y * ZC + i, x)
-
-    def xy_dev(i):
-        return (lax.rem(i, Y) * ZC + zc, i // Y)
+    def zc_dev(d):
+        return (y * ZC + d, x)
+
+    def xy_dev(x2, y2):
+        return (y2 * ZC + zc, x2)
 
     me_xy = x * Y + y
+
+    xs = [wrap(x + dx, X) for dx in range(X)]
+
+    def each_zc(do):
+        do(wrap(zc + ZC // 2, ZC))
+
+        def pair(i, _):
+            do(wrap(zc + (ZC // 2 - i), ZC))
+            do(wrap(zc - (ZC // 2 - i), ZC))
+            return 0
+
+        lax.fori_loop(1, ZC // 2, pair, 0)
+
+    def each_xy(do):
+        def row(y2, dxs):
+            for dx in dxs:
+                do(xs[dx], y2)
+
+        row(wrap(y + Y // 2, Y), (2, 1, 3, 0))
+
+        def pair(i, _):
+            row(wrap(y + (Y // 2 - i), Y), (2, 1, 3, 0))
+            row(wrap(y - (Y // 2 - i), Y), (2, 1, 3, 0))
+            return 0
+
+        lax.fori_loop(1, Y // 2, pair, 0)
+        row(y, (2, 1, 3))
+
     before = (lax.rem(chan + C - 1, C), x)
     after = (lax.rem(chan + 1, C), x)
 
@@ -111,25 +145,26 @@
         loads.append(pltpu.make_async_copy(rec_hbm.at[:, cols], raw.at[:, cols], local_sem.at[n]))
     load_fwd = pltpu.make_async_copy(fwd_hbm, fwd, local_sem.at[NB])
     load_lag = pltpu.make_async_copy(lag_hbm, lagt, local_sem.at[NB + 1])
-    for c in loads:
+    small = [
+        pltpu.make_async_copy(src, dst, small_sem.at[n])
+        for n, (src, dst) in enumerate((
+            (taps_hbm, taps_ref), (off_hbm, off_ref), (part_hbm, part_ref), (count_hbm, count_ref),
+        ))
+    ]
+    for c in small + loads:
         c.start()
     load_fwd.start()
     load_lag.start()
 
     barrier = pltpu.get_barrier_semaphore()
 
-    def signal_zc(i, _):
-        pl.semaphore_signal(barrier, inc=1, device_id=zc_dev(lax.rem(zc + i, ZC)), device_id_type=MESH)
-        return 0
-
-    def signal_xy(i, _):
-        pl.semaphore_signal(barrier, inc=1, device_id=xy_dev(lax.rem(me_xy + i, XY)), device_id_type=MESH)
-        return 0
-
-    lax.fori_loop(1, ZC, signal_zc, 0)
-    lax.fori_loop(1, XY, signal_xy, 0)
-    pl.semaphore_signal(barrier, inc=1, device_id=before, device_id_type=MESH)
-    pl.semaphore_signal(barrier, inc=1, device_id=after, device_id_type=MESH)
+    def signal(device):
+        pl.semaphore_signal(barrier, inc=1, device_id=device, device_id_type=MESH)
+
+    each_zc(lambda d: signal(zc_dev(d)))
+    each_xy(lambda x2, y2: signal(xy_dev(x2, y2)))
+    signal(before)
+    signal(after)
 
     r = iota((BINS, BINS), 0)
     c = iota((BINS, BINS), 1)
@@ -142,6 +177,7 @@
 
     place = (iota((TAPS, WIN), 1) == 67 + TAPS - iota((TAPS, WIN), 0))
     place = jnp.where(place, 1.0, 0.0).astype(BF)
+    small[0].wait()
     t_hi, t_lo = halves(jnp.broadcast_to(taps_ref[...], (8, TAPS)))
     row_hi = jnp.broadcast_to(dot(t_hi, place)[0:1], (QB, WIN))
     row_lo = jnp.broadcast_to(dot(t_lo, place)[0:1], (QB, WIN))
@@ -226,29 +262,27 @@
     white_b[...] = dot(perm[...], wim).astype(BF)
 
     def send_zc(src, dst, k):
-        def body(i, _):
-            d = lax.rem(zc + i, ZC)
+        mine = pl.ds(pl.multiple_of(zc * XY, XY), XY)
+
+        def one(d):
             pltpu.make_async_remote_copy(
-                src.at[pl.ds(d * XY, XY)], dst.at[pl.ds(zc * XY, XY)], ssem.at[k], rsem.at[k],
+                src.at[pl.ds(pl.multiple_of(d * XY, XY), XY)], dst.at[mine], ssem.at[k], rsem.at[k],
                 device_id=zc_dev(d), device_id_type=MESH,
             ).start()
-            return 0
-
-        lax.fori_loop(1, ZC, body, 0)
-        mine = pl.ds(pl.multiple_of(zc * XY, XY), XY)
+
+        each_zc(one)
         dst[mine, :] = src[mine, :]
 
     def send_xy(src, dst, k):
-        def body(i, _):
-            d = lax.rem(me_xy + i, XY)
+        mine = pl.ds(pl.multiple_of(me_xy * ZC, ZC), ZC)
+
+        def one(x2, y2):
             pltpu.make_async_remote_copy(
-                src.at[pl.ds(d * ZC, ZC)], dst.at[pl.ds(me_xy * ZC, ZC)], ssem.at[k], rsem.at[k],
-                device_id=xy_dev(d), device_id_type=MESH,
+                src.at[pl.ds(pl.multiple_of((x2 * Y + y2) * ZC, ZC), ZC)], dst.at[mine], ssem.at[k], rsem.at[k],
+                device_id=xy_dev(x2, y2), device_id_type=MESH,
             ).start()
-            return 0
-
-        lax.fori_loop(1, XY, body, 0)
-        mine = pl.ds(pl.multiple_of(me_xy * ZC, ZC), ZC)
+
+        each_xy(one)
         dst[mine, :] = src[mine, :]
 
     def done(ref, sems, k, count):
@@ -280,6 +314,8 @@
     to_before.wait()
     to_after.wait()
     load_lag.wait()
+    for c in small[1:]:
+        c.wait()
 
     def near(o, _):
         off = off_ref[o]
@@ -340,20 +376,21 @@
     done(b3, rsem, 3, zc_rows)
     wi[...] = dot(perm[...], b3[...]).astype(BF)
 
-    loop_r = [jnp.zeros((C, C), F32) for _ in range(MAXLB)]
-    loop_i = [jnp.zeros((C, C), F32) for _ in range(MAXLB)]
+    far = []
+    own = []
     for s in range(SEGS):
-        own_r = wr[s * C : (s + 1) * C, :]
-        own_i = wi[s * C : (s + 1) * C, :]
-        far_r = dot(pick, dot(own_r, flip).astype(BF))
-        far_i = dot(pick, dot(own_i, flip).astype(BF))
-        own_r = own_r.astype(F32)
-        own_i = own_i.astype(F32)
-        for k in range(MAXLB):
-            pr = far_r[k * C : (k + 1) * C, :]
-            pi = far_i[k * C : (k + 1) * C, :]
-            loop_r[k] = loop_r[k] + own_r * pr + own_i * pi
-            loop_i[k] = loop_i[k] + own_i * pr - own_r * pi
+        pair = (wr[s * C : (s + 1) * C, :], wi[s * C : (s + 1) * C, :])
+        far.append(tuple(dot(pick, dot(v, flip).astype(BF)) for v in pair))
+        own.append(tuple(v.astype(F32) for v in pair))
+
+    def loop_spec(k):
+        real, imag = jnp.zeros((C, C), F32), jnp.zeros((C, C), F32)
+        for s in range(SEGS):
+            own_r, own_i = own[s]
+            pr, pi = (v[k * C : (k + 1) * C, :] for v in far[s])
+            real = real + own_r * pr + own_i * pi
+            imag = imag + own_i * pr - own_r * pi
+        return real, imag
 
     def gather_lanes(parts, q):
         out = jnp.zeros((C, C), F32)
@@ -362,17 +399,18 @@
             out = jnp.where((lane_b >= 32 * j) & (lane_b < 32 * (j + 1)), turned, out)
         return out.astype(BF)
 
-    for q in range(X):
-        rows = slice(q * C, (q + 1) * C)
-        back_a[rows, :] = gather_lanes([loop_r[0], loop_i[0], loop_r[1], loop_i[1]], q)
-        back_b[rows, :] = gather_lanes([loop_r[2], loop_i[2]], q)
-
     done(a2, ssem, 2, xy_rows)
     done(b2, ssem, 3, zc_rows)
     done(white_a, ssem, 0, zc_rows)
     done(white_b, ssem, 1, xy_rows)
+    first = loop_spec(0) + loop_spec(1)
+    for q in range(X):
+        back_a[q * C : (q + 1) * C, :] = gather_lanes(first, q)
     a3[...] = dot(permt[...], back_a[...]).astype(BF)
     send_zc(a3, a4, 4)
+    second = loop_spec(2)
+    for q in range(X):
+        back_b[q * C : (q + 1) * C, :] = gather_lanes(second, q)
     send_xy(back_b, b4, 5)
 
     three = near_recv.at[pl.ds(0, X - 1)]
@@ -412,12 +450,16 @@
     done(b2, ssem, 7, zc_rows)
 
 
+def write_out(near_ref, loop_ref, near_out, loop_out):
+    near_out[:, 0, :] = near_ref[...]
+    loop_out[0] = loop_ref[...]
+
+
 def body(recording, filter_taps, offsets, loop_partner, loop_count):
     fwd = jnp.asarray(forward_tables())
     lagt = jnp.asarray(lag_tables())
     vmem = pl.BlockSpec(memory_space=pltpu.VMEM)
-    hbm = pl.BlockSpec(memory_space=pl.ANY)
-    smem = pl.BlockSpec(memory_space=pltpu.SMEM)
+    hbm = pl.BlockSpec(memory_space=pltpu.HBM)
     rows = pltpu.VMEM((BINS, C), BF)
     dma = pltpu.SemaphoreType.DMA
     near, loop = pl.pallas_call(
@@ -426,9 +468,13 @@
             jax.ShapeDtypeStruct((C, LAGS), F32),
             jax.ShapeDtypeStruct((MAXLB, C // X, LAGS), F32),
         ),
-        in_specs=[smem, hbm, vmem, vmem, vmem, hbm, hbm],
+        in_specs=[hbm] * 7,
         out_specs=(vmem, vmem),
         scratch_shapes=[
+            pltpu.SMEM((NOFF,), jnp.int32),
+            pltpu.VMEM((1, TAPS), F32),
+            pltpu.VMEM((MAXLB, C), jnp.int32),
+            pltpu.VMEM((1, C), jnp.int32),
             pltpu.VMEM((C, NFFT * DECIM), F32),
             pltpu.VMEM((2 * C, RIM + NFFT * DECIM), BF),
             pltpu.VMEM((NFFT, C), F32),
@@ -449,14 +495,26 @@
             pltpu.VMEM((NOFF, LAGS, C), BF),
             pltpu.VMEM((X - 1, LAGS, C), BF),
             rows, rows,
-            dma((NB + 2,)), dma((2,)), dma((4,)), dma((2,)), dma((8,)), dma((8,)),
+            dma((NB + 2,)), dma((4,)), dma((2,)), dma((4,)), dma((2,)), dma((8,)), dma((8,)),
         ],
-        compiler_params=pltpu.CompilerParams(collective_id=0, has_side_effects=True),
-    )(
-        offsets, recording, filter_taps.reshape(1, TAPS), loop_partner.T,
-        loop_count.reshape(1, C), fwd, lagt,
-    )
-    return near[:, None, :], loop[None]
+        compiler_params=pltpu.CompilerParams(collective_id=0, has_side_effects=True, vmem_limit_bytes=32 << 20),
+    )(*(
+        pltpu.with_memory_space_constraint(v, pltpu.HBM)
+        for v in (
+            offsets, recording, filter_taps.reshape(1, TAPS), loop_partner.T,
+            loop_count.reshape(1, C), fwd, lagt,
+        )
+    ))
+    return pl.pallas_call(
+        write_out,
+        out_shape=(
+            jax.ShapeDtypeStruct((C, 1, LAGS), F32),
+            jax.ShapeDtypeStruct((1, MAXLB, C // X, LAGS), F32),
+        ),
+        in_specs=[vmem, vmem],
+        out_specs=(vmem, vmem),
+        compiler_params=pltpu.CompilerParams(vmem_limit_bytes=4 << 20),
+    )(near, loop)
 
 
 def solution(mesh):

time: 58.4 us -> 52.2 us (0.89)
  local copies, waits for them, and re-layouts: 3.23 us -> 0 us
  Pallas kernels: 54.3 us -> 51.5 us
    pallas_call x1, Pallas kernels: 54.3 us -> 50.8 us  [body(): pl.pallas_call(kernel, out_shape=(jax.ShapeDtypeStruct((C, LAGS), F32), j...]
    unnamed x2 -> x0, local copies, waits for them, and re-layouts: 3.23 us -> none
    pallas_call x0 -> x1, Pallas kernels: none -> 0.71 us  [body(): pl.pallas_call(write_out, out_shape=(jax.ShapeDtypeStruct((C, 1, LAGS), F...]
where the time goes in v2:
time: 52.2 us; the launch traced here: 52.1 us
  Pallas kernels  51.5 us (99%)
  between operations  0.64 us (1%)
    pallas_call x1, Pallas kernels, body(): pl.pallas_call(kernel, out_shape=(jax.ShapeDtypeStruct((C, LAGS), F32), j...  50.8 us

profile of v2, /device:TPU:1, one launch (start us, length us, event | category | flops | bytes accessed | tf_op | source)
XLA Modules:
  0.0 52.1 jit_solution(6151542462521088749)
XLA Ops:
  0.6 50.8 %shard_map.86 = (f32[128,256]{1,0:T(8,128)S(1)}, f32[3,32,256]{2,1,0:T(8,128)S(1)}) custom-call(s32[4]{0:T(128)} %off_hbm.1, f32[128,4096]{1,0:T(8,128)} %rec_hbm.1, f32[1,64]{1,0:T(1,128)} %bitcast.4, s32[3,128]{1,0:T(4,128)} %bitcast.3, s32[1,128]{1,0:T(1,128)} %bitcast.5, bf16[4,512,512]{2,1,0:T(8,128)(2,1)} %constant.4.clone.fwd_hbm, ...), custom_call_target="tpu_custom_call" | custom-call | tf_op jit(solution)/shard_map/pallas_call | solution.py:465
  51.4 0.7 %shard_map.87 = (f32[128,1,256]{2,1,0:T(1,128)}, f32[1,3,32,256]{3,2,1,0:T(8,128)}) custom-call(f32[128,256]{1,0:T(8,128)S(1)} %get-tuple-element.4.near_ref, f32[3,32,256]{2,1,0:T(8,128)S(1)} %get-tuple-element.5.loop_ref), custom_call_target="tpu_custom_call" | custom-call | tf_op jit(solution)/shard_map/pallas_call | solution.py:508

commit v3 on v2

--- a/solution.py
+++ b/solution.py
@@ -92,7 +92,7 @@
     off_hbm, rec_hbm, taps_hbm, part_hbm, count_hbm, fwd_hbm, lag_hbm,
     near_out, loop_out,
     off_ref, taps_ref, part_ref, count_ref,
-    raw, rec, dec, fwd, lagt, perm, permt, band, rim_send, rim_recv,
+    raw, rec, dec, fwd, lagt, lagp, perm, permt, band, rim_send, rim_recv,
     spec, uv, white_a, white_b, halo_send, halo_recv,
     a1, a2, a3, b1, b2, b3, wr, wi, a4, a5, b4, b5, near_part, near_send, near_recv, back_a, back_b,
     local_sem, small_sem, rim_sem, halo_sem, near_sem, ssem, rsem,
@@ -311,12 +311,6 @@
     )
     to_before.start()
     to_after.start()
-    to_before.wait()
-    to_after.wait()
-    load_lag.wait()
-    for c in small[1:]:
-        c.wait()
-
     def near(o, _):
         off = off_ref[o]
         own_r = white_a[...].astype(F32)
@@ -341,8 +335,6 @@
         near_send[o] = out.astype(BF)
         return 0
 
-    lax.fori_loop(0, 2, near, 0)
-
     done(a1, rsem, 0, zc_rows)
     a2[...] = dot(perm[...], a1[...]).astype(BF)
     send_xy(a2, wr, 2)
@@ -350,7 +342,12 @@
     b2[...] = dot(permt[...], b1[...]).astype(BF)
     send_zc(b2, b3, 3)
 
-    lax.fori_loop(2, NOFF, near, 0)
+    to_before.wait()
+    to_after.wait()
+    load_lag.wait()
+    for c in small[1:]:
+        c.wait()
+    lax.fori_loop(0, NOFF, near, 0)
 
     def near_to(i, k):
         d = lax.rem(x + i, X)
@@ -372,22 +369,21 @@
         picks.append(jnp.where(column == lane_b.astype(F32), 1.0, 0.0).astype(BF))
     pick = jnp.concatenate(picks, axis=0)
 
+    def pick_far(w):
+        parts = [w[s * C : (s + 1) * C, :] for s in range(SEGS)]
+        return [v.astype(F32) for v in parts], [dot(pick, dot(v, flip).astype(BF)) for v in parts]
+
     done(wr, rsem, 2, xy_rows)
+    own_re, far_re = pick_far(wr)
     done(b3, rsem, 3, zc_rows)
     wi[...] = dot(perm[...], b3[...]).astype(BF)
-
-    far = []
-    own = []
-    for s in range(SEGS):
-        pair = (wr[s * C : (s + 1) * C, :], wi[s * C : (s + 1) * C, :])
-        far.append(tuple(dot(pick, dot(v, flip).astype(BF)) for v in pair))
-        own.append(tuple(v.astype(F32) for v in pair))
+    own_im, far_im = pick_far(wi)
 
     def loop_spec(k):
         real, imag = jnp.zeros((C, C), F32), jnp.zeros((C, C), F32)
         for s in range(SEGS):
-            own_r, own_i = own[s]
-            pr, pi = (v[k * C : (k + 1) * C, :] for v in far[s])
+            own_r, own_i = own_re[s], own_im[s]
+            pr, pi = (v[s][k * C : (k + 1) * C, :] for v in (far_re, far_im))
             real = real + own_r * pr + own_i * pi
             imag = imag + own_i * pr - own_r * pi
         return real, imag
@@ -419,6 +415,9 @@
     for i in range(X - 1):
         total = total + near_recv[i].astype(F32)
     near_out[...] = jnp.transpose(total)
+    for n in range(2):
+        for k in range(2):
+            lagp[n, :, k * BINS : (k + 1) * BINS] = dot(lagt[n, :, k * BINS : (k + 1) * BINS], permt[...]).astype(BF)
 
     done(a4, rsem, 4, zc_rows)
     a2[...] = dot(perm[...], a4[...]).astype(BF)
@@ -428,20 +427,19 @@
     send_zc(b2, b5, 7)
 
     done(a5, rsem, 6, xy_rows)
-    got_a = dot(permt[...], a5[...]).astype(BF)
-    lag_r = dot(lagt[0, :, :BINS], got_a) + dot(lagt[1, :, :BINS], got_a)
-    lag_i = dot(lagt[0, :, BINS:], got_a) + dot(lagt[1, :, BINS:], got_a)
-    lag_r = jnp.transpose(lag_r)
-    lag_i = jnp.transpose(lag_i)
-    loop_out[0] = lag_r[0:32] + lag_i[32:64]
-    loop_out[1] = lag_r[64:96] + lag_i[96:128]
+    def lags(table, got):
+        real = dot(table[0, :, :BINS], got) + dot(table[1, :, :BINS], got)
+        imag = dot(table[0, :, BINS:], got) + dot(table[1, :, BINS:], got)
+        return real + pltpu.roll(imag, C - 32, 1)
+
+    lag_a = lags(lagp, a5[...])
     done(b5, rsem, 7, zc_rows)
-    got_b = b5[...]
-    lag_r = dot(lagt[0, :, :BINS], got_b) + dot(lagt[1, :, :BINS], got_b)
-    lag_i = dot(lagt[0, :, BINS:], got_b) + dot(lagt[1, :, BINS:], got_b)
-    lag_r = jnp.transpose(lag_r)
-    lag_i = jnp.transpose(lag_i)
-    loop_out[2] = lag_r[0:32] + lag_i[32:64]
+    lag_b = pltpu.roll(lags(lagt, b5[...]), 32, 1)
+    lane_l = iota((LAGS, C), 1)
+    both = jnp.transpose(jnp.where((lane_l >= 32) & (lane_l < 64), lag_b, lag_a))
+    loop_out[0] = both[0:32]
+    loop_out[1] = both[64:96]
+    loop_out[2] = both[32:64]
 
     pltpu.make_async_copy(three, three, near_sem.at[0]).wait()
     done(a3, ssem, 4, zc_rows)
@@ -479,6 +477,7 @@
             pltpu.VMEM((2 * C, RIM + NFFT * DECIM), BF),
             pltpu.VMEM((NFFT, C), F32),
             pltpu.VMEM((4, BINS, NFFT // 2), BF),
+            pltpu.VMEM((2, LAGS, 2 * BINS), BF),
             pltpu.VMEM((2, LAGS, 2 * BINS), BF),
             pltpu.VMEM((BINS, BINS), BF),
             pltpu.VMEM((BINS, BINS), BF),

time: 52.2 us -> 50.3 us (0.964)
  Pallas kernels: 51.5 us -> 49.6 us
    pallas_call x1, Pallas kernels: 50.8 us -> 48.9 us  [body(): pl.pallas_call(kernel, out_shape=(jax.ShapeDtypeStruct((C, LAGS), F32), j...]
where the time goes in v3:
time: 50.3 us; the launch traced here: 50.2 us
  Pallas kernels  49.6 us (99%)
  between operations  0.64 us (1%)
    pallas_call x1, Pallas kernels, body(): pl.pallas_call(kernel, out_shape=(jax.ShapeDtypeStruct((C, LAGS), F32), j...  48.9 us

profile of v3, /device:TPU:1, one launch (start us, length us, event | category | flops | bytes accessed | tf_op | source)
XLA Modules:
  0.0 50.2 jit_solution(5345417205151064272)
XLA Ops:
  0.6 48.9 %shard_map.86 = (f32[128,256]{1,0:T(8,128)S(1)}, f32[3,32,256]{2,1,0:T(8,128)S(1)}) custom-call(s32[4]{0:T(128)} %off_hbm.1, f32[128,4096]{1,0:T(8,128)} %rec_hbm.1, f32[1,64]{1,0:T(1,128)} %bitcast.4, s32[3,128]{1,0:T(4,128)} %bitcast.3, s32[1,128]{1,0:T(1,128)} %bitcast.5, bf16[4,512,512]{2,1,0:T(8,128)(2,1)} %constant.4.clone.fwd_hbm, ...), custom_call_target="tpu_custom_call" | custom-call | tf_op jit(solution)/shard_map/pallas_call | solution.py:463
  49.5 0.7 %shard_map.87 = (f32[128,1,256]{2,1,0:T(1,128)}, f32[1,3,32,256]{3,2,1,0:T(8,128)}) custom-call(f32[128,256]{1,0:T(8,128)S(1)} %get-tuple-element.4.near_ref, f32[3,32,256]{2,1,0:T(8,128)S(1)} %get-tuple-element.5.loop_ref), custom_call_target="tpu_custom_call" | custom-call | tf_op jit(solution)/shard_map/pallas_call | solution.py:507
